TPU v7x, 32 devices: a whole 2x2x4 slice. The times are simulated.
32 devices in a mesh: dp: 8 (over z, y), tensor: 4 (over x, core).
Axes of the slice: x: 2, y: 2, z: 4, core: 2. Of those that a mesh axis runs over, the one named last changes fastest.
Arguments:
- tokens: bfloat16 [8192, 1024], P(('dp', 'tensor')), may hold values from -6 to 6
- cotangent: float32 [8192, 1024], P(('dp', 'tensor')), may hold values from -6 to 6
- lengths: int32 [8, 2], P('dp'), may hold values from 64 to 512, as said below
- order: int32 [8, 1024], P('dp'), may hold values from 0 to 1023, each once within a row
- adapter_ids: int32 [8, 2], P('dp'), may hold values from 0 to 7
- norm1_gain: float32 [1024], replicated, may hold values from 0.25 to 1.75
- norm1_shift: float32 [1024], replicated, may hold values from -1.5 to 1.5
- qkv_weight: bfloat16 [1024, 3, 1024], P(None, None, 'tensor'), may hold values from -0.1875 to 0.1875
- qv_bias: float32 [2, 1024], P(None, 'tensor'), may hold values from -1.5 to 1.5
- proj_weight: bfloat16 [1024, 1024], P('tensor'), may hold values from -1.5 to 1.5
- proj_bias: float32 [1024], replicated, may hold values from -1.5 to 1.5
- norm2_gain: float32 [1024], replicated, may hold values from 0.25 to 1.75
- norm2_shift: float32 [1024], replicated, may hold values from -1.5 to 1.5
- up_weight: bfloat16 [1024, 4096], P(None, 'tensor'), may hold values from -0.1875 to 0.1875
- up_bias: float32 [4096], P('tensor'), may hold values from -1.5 to 1.5
- down_weight: bfloat16 [4096, 1024], P('tensor'), may hold values from -0.09375 to 0.09375
- down_bias: float32 [1024], replicated, may hold values from -1.5 to 1.5
- adapt_qkv_in: bfloat16 [1024, 128], replicated, may hold values from -0.1875 to 0.1875
- adapt_qkv_out: bfloat16 [128, 3, 1024], P(None, None, 'tensor'), may hold values from -0.75 to 0.75
- adapt_proj_in: bfloat16 [1024, 128], P('tensor'), may hold values from -0.75 to 0.75
- adapt_proj_out: bfloat16 [128, 1024], replicated, may hold values from -0.75 to 0.75
- adapt_up_in: bfloat16 [1024, 128], replicated, may hold values from -0.1875 to 0.1875
- adapt_up_out: bfloat16 [128, 4096], P(None, 'tensor'), may hold values from -0.75 to 0.75
- adapt_down_in: bfloat16 [4096, 128], P('tensor'), may hold values from -0.09375 to 0.09375
- adapt_down_out: bfloat16 [128, 1024], replicated, may hold values from -0.75 to 0.75
Outputs:
- result: float32 [8192, 1024], P(('dp', 'tensor'))
- grad_input: float32 [8192, 1024], P(('dp', 'tensor'))
- grad_qkv_in: float32 [1024, 128], replicated
- grad_qkv_out: float32 [128, 3, 1024], P(None, None, 'tensor')
- grad_proj_in: float32 [1024, 128], P('tensor')
- grad_proj_out: float32 [128, 1024], replicated
- grad_up_in: float32 [1024, 128], replicated
- grad_up_out: float32 [128, 4096], P(None, 'tensor')
- grad_down_in: float32 [4096, 128], P('tensor')
- grad_down_out: float32 [128, 1024], replicated
Inputs may be any that keep to these rules, and one draw needn't show every extreme that they name: `lengths`: in every group one sequence has exactly 512 valid tokens; the others have at least 512 // 8 (and at least one). `order`: each row is a permutation of the group's 1024 stored rows.
All inputs are finite; a program needn't handle non-finite values.
Results may differ from a plain program's by a relative error of at most 0.023.
Values may be sent and summed in bfloat16 or wider, within the bound.
No kernel may reach another device: no remote copies, remote signals or barrier semaphores. Data moves between devices by JAX's collectives and lax.ppermute only.
A program may use at most 128 MiB of HBM per device.

v0:
```python
import math
import jax
import jax.numpy as jnp
from jax import lax
from jax.sharding import PartitionSpec as P

D = 1024
HD = 64
RANK = 16
EPSILON = 1e-05
NEGATIVE = -1000000000.0


def layer_norm(values, gain, shift):
    centre = values - jnp.mean(values, -1, keepdims=True)
    spread = jnp.mean(centre * centre, -1, keepdims=True)
    return centre * lax.rsqrt(spread + EPSILON) * gain + shift


def matmul(left, right):
    return jnp.dot(left, right, preferred_element_type=jnp.float32)


def matmul_back(left, right):
    return lax.dot_general(
        left, right, (((1,), (1,)), ((), ())), preferred_element_type=jnp.float32
    )


def matmul_over(left, right):
    return lax.dot_general(
        left, right, (((0,), (0,)), ((), ())), preferred_element_type=jnp.float32
    )


def gelu_tanh(values):
    return jax.nn.gelu(values, approximate=True)


def block_scores(queries, keys, query_start, length):
    scale = 1.0 / math.sqrt(HD)
    scores = jnp.einsum("qhc,khc->hqk", queries, keys, preferred_element_type=jnp.float32) * scale
    query_pos = query_start + jnp.arange(queries.shape[0], dtype=jnp.int32)
    key_pos = jnp.arange(keys.shape[0], dtype=jnp.int32)
    allowed = (key_pos[None, :] <= query_pos[:, None]) & (key_pos[None, :] < length)
    return jnp.where(allowed[None], scores, NEGATIVE)


def attention_forward(qkv_seq, lengths_row, seq_len):
    group_rows = qkv_seq.shape[0]
    heads_here = qkv_seq.shape[2] // HD
    block_rows = min(512, seq_len)
    per_seq = seq_len // block_rows
    split = qkv_seq.reshape(group_rows, 3, heads_here, HD)

    def one_block(block_id):
        seq_id = block_id // per_seq
        query_start = block_id % per_seq * block_rows
        base = seq_id * seq_len
        queries = lax.dynamic_slice_in_dim(split[:, 0], base + query_start, block_rows, 0)
        keys = lax.dynamic_slice_in_dim(split[:, 1], base, seq_len, 0)
        values = lax.dynamic_slice_in_dim(split[:, 2], base, seq_len, 0)
        scores = block_scores(queries, keys, query_start, lengths_row[seq_id])
        top = jnp.max(scores, -1, keepdims=True)
        weights = jnp.exp(scores - top)
        total = jnp.sum(weights, -1, keepdims=True)
        probs = (weights / total).astype(jnp.bfloat16)
        attended = jnp.einsum("hqk,khc->qhc", probs, values, preferred_element_type=jnp.float32)
        return (attended.reshape(block_rows, heads_here * HD), (top + jnp.log(total))[..., 0])

    blocks = group_rows // block_rows
    outputs, log_totals = lax.map(one_block, jnp.arange(blocks, dtype=jnp.int32))
    return (outputs.reshape(group_rows, heads_here * HD), log_totals)


def attention_backward(qkv_seq, grad_seq, log_totals, lengths_row, seq_len):
    group_rows = qkv_seq.shape[0]
    heads_here = qkv_seq.shape[2] // HD
    block_rows = min(512, seq_len)
    per_seq = seq_len // block_rows
    seqs = group_rows // seq_len
    scale = 1.0 / math.sqrt(HD)
    split = qkv_seq.reshape(group_rows, 3, heads_here, HD)
    grad_split = grad_seq.reshape(group_rows, heads_here, HD)

    def one_block(block_id):
        seq_id = block_id // per_seq
        query_start = block_id % per_seq * block_rows
        base = seq_id * seq_len
        queries = lax.dynamic_slice_in_dim(split[:, 0], base + query_start, block_rows, 0)
        keys = lax.dynamic_slice_in_dim(split[:, 1], base, seq_len, 0)
        values = lax.dynamic_slice_in_dim(split[:, 2], base, seq_len, 0)
        grad_block = lax.dynamic_slice_in_dim(grad_split, base + query_start, block_rows, 0)
        scores = block_scores(queries, keys, query_start, lengths_row[seq_id])
        probs = jnp.exp(scores - log_totals[block_id][..., None])
        grad_probs = jnp.einsum(
            "qhc,khc->hqk", grad_block, values, preferred_element_type=jnp.float32
        )
        centre = jnp.sum(probs * grad_probs, -1, keepdims=True)
        grad_raw = (probs * (grad_probs - centre) * scale).astype(jnp.bfloat16)
        grad_query = jnp.einsum("hqk,khc->qhc", grad_raw, keys, preferred_element_type=jnp.float32)
        grad_key = jnp.einsum("hqk,qhc->khc", grad_raw, queries, preferred_element_type=jnp.float32)
        grad_value = jnp.einsum(
            "hqk,qhc->khc",
            probs.astype(jnp.bfloat16),
            grad_block,
            preferred_element_type=jnp.float32,
        )
        return (grad_query, grad_key, grad_value)

    blocks = group_rows // block_rows
    grad_query, grad_key, grad_value = lax.map(one_block, jnp.arange(blocks, dtype=jnp.int32))
    width_here = heads_here * HD
    grad_query = grad_query.reshape(group_rows, width_here)
    grad_key = jnp.sum(grad_key.reshape(seqs, per_seq, seq_len, width_here), axis=1).reshape(
        group_rows, width_here
    )
    grad_value = jnp.sum(grad_value.reshape(seqs, per_seq, seq_len, width_here), axis=1).reshape(
        group_rows, width_here
    )
    return jnp.stack([grad_query, grad_key, grad_value], 1)


def body(
    tokens,
    cotangent,
    lengths,
    order,
    adapter_ids,
    norm1_gain,
    norm1_shift,
    qkv_weight,
    qv_bias,
    proj_weight,
    proj_bias,
    norm2_gain,
    norm2_shift,
    up_weight,
    up_bias,
    down_weight,
    down_bias,
    adapt_qkv_in,
    adapt_qkv_out,
    adapt_proj_in,
    adapt_proj_out,
    adapt_up_in,
    adapt_up_out,
    adapt_down_in,
    adapt_down_out,
):
    own_rows = tokens.shape[0]
    order_row = order[0]
    lengths_row = lengths[0]
    ids_row = adapter_ids[0]
    group_rows = order_row.shape[0]
    seqs = lengths_row.shape[0]
    seq_len = group_rows // seqs
    adapt_cols = adapt_qkv_in.shape[1]
    rank_index = lax.axis_index("tensor")
    inverse = (
        jnp.zeros((group_rows,), jnp.int32)
        .at[order_row]
        .set(jnp.arange(group_rows, dtype=jnp.int32))
    )
    seq_of = inverse // seq_len
    adapter_of = jnp.sum(
        jnp.where(
            seq_of[:, None] == jnp.arange(seqs, dtype=jnp.int32)[None, :], ids_row[None, :], 0
        ),
        axis=1,
    )
    group_mask = (
        jnp.arange(adapt_cols, dtype=jnp.int32)[None, :] // RANK == adapter_of[:, None]
    ).astype(jnp.float32)
    own_mask = lax.dynamic_slice_in_dim(group_mask, rank_index * own_rows, own_rows, 0)
    bias_three = jnp.stack([qv_bias[0], jnp.zeros_like(qv_bias[0]), qv_bias[1]])
    proj_joined = jnp.concatenate([proj_weight, adapt_proj_in], 1)
    down_joined = jnp.concatenate([down_weight, adapt_down_in], 1)
    up_joined = jnp.concatenate([up_weight, adapt_up_out], 0)
    qkv_joined = jnp.concatenate([qkv_weight, adapt_qkv_out], 0)

    def project_qkv(rows_all, lowrank_all):
        value = jnp.einsum("rd,dkc->rkc", rows_all, qkv_weight, preferred_element_type=jnp.float32)
        value = value + jnp.einsum(
            "ra,akc->rkc", lowrank_all, adapt_qkv_out, preferred_element_type=jnp.float32
        )
        return (value + bias_three[None]).astype(jnp.bfloat16)

    def project_up(rows_all, lowrank_all):
        return matmul(rows_all, up_weight) + matmul(lowrank_all, adapt_up_out) + up_bias

    inputs = tokens.astype(jnp.float32)
    normed1 = layer_norm(inputs, norm1_gain, norm1_shift).astype(jnp.bfloat16)
    low1 = (matmul(normed1, adapt_qkv_in) * own_mask).astype(jnp.bfloat16)
    normed1_all, low1_small = (
        lax.all_gather(normed1, "tensor", axis=0, tiled=True),
        lax.all_gather(low1, "tensor", axis=0, tiled=True),
    )
    low1_all = low1_small
    qkv_arr = project_qkv(normed1_all, low1_all)
    qkv_seq = jnp.take(qkv_arr, order_row, axis=0)
    attended_seq, log_totals = attention_forward(qkv_seq, lengths_row, seq_len)
    attended = jnp.take(attended_seq.astype(jnp.bfloat16), inverse, axis=0)
    rows = attended
    mask_rows = group_mask
    part = matmul(rows, proj_joined)
    summed_attn = lax.psum_scatter(
        jnp.concatenate([part[:, :D], part[:, D:] * mask_rows], 1).astype(jnp.bfloat16),
        "tensor",
        scatter_dimension=0,
        tiled=True,
    ).astype(jnp.float32)
    proj_low = summed_attn[:, D:].astype(jnp.bfloat16)
    mid = inputs + summed_attn[:, :D] + matmul(proj_low, adapt_proj_out) + proj_bias
    normed2 = layer_norm(mid, norm2_gain, norm2_shift).astype(jnp.bfloat16)
    low2 = (matmul(normed2, adapt_up_in) * own_mask).astype(jnp.bfloat16)
    normed2_all, low2_small = (
        lax.all_gather(normed2, "tensor", axis=0, tiled=True),
        lax.all_gather(low2, "tensor", axis=0, tiled=True),
    )
    low2_all = low2_small
    upper = project_up(normed2_all, low2_all)
    active = gelu_tanh(upper).astype(jnp.bfloat16)
    rows = active
    mask_rows = group_mask
    part = matmul(rows, down_joined)
    summed_mlp = lax.psum_scatter(
        jnp.concatenate([part[:, :D], part[:, D:] * mask_rows], 1).astype(jnp.bfloat16),
        "tensor",
        scatter_dimension=0,
        tiled=True,
    ).astype(jnp.float32)
    down_low = summed_mlp[:, D:].astype(jnp.bfloat16)
    result = mid + summed_mlp[:, :D] + matmul(down_low, adapt_down_out) + down_bias
    grad_mlp = cotangent.astype(jnp.bfloat16)
    grad_down_low = (matmul_back(grad_mlp, adapt_down_out) * own_mask).astype(jnp.bfloat16)
    grad_down_out_part = matmul_over(down_low, grad_mlp)
    grad_mlp_all, grad_down_small = (
        lax.all_gather(grad_mlp, "tensor", axis=0, tiled=True),
        lax.all_gather(grad_down_low, "tensor", axis=0, tiled=True),
    )
    normed2_again, low2_again_small = (
        lax.all_gather(normed2, "tensor", axis=0, tiled=True),
        lax.all_gather(low2, "tensor", axis=0, tiled=True),
    )
    upper = project_up(normed2_again, low2_again_small)
    active = gelu_tanh(upper).astype(jnp.bfloat16)
    low2_all = low2_again_small
    grad_active = matmul_back(grad_mlp_all, down_weight) + matmul_back(
        grad_down_small, adapt_down_in
    )
    grad_down_in_part = matmul_over(active, grad_down_small)
    gelu_value, gelu_pull = jax.vjp(gelu_tanh, upper)
    grad_upper = gelu_pull(grad_active)[0].astype(jnp.bfloat16)
    grad_up_out_part = matmul_over(low2_all, grad_upper)
    rows = grad_upper
    part = matmul_back(rows, up_joined)
    summed_up = lax.psum_scatter(
        jnp.concatenate([part[:, :D], part[:, D:]], 1).astype(jnp.bfloat16),
        "tensor",
        scatter_dimension=0,
        tiled=True,
    ).astype(jnp.float32)
    grad_low2 = (summed_up[:, D:] * own_mask).astype(jnp.bfloat16)
    grad_up_in_part = matmul_over(normed2, grad_low2)
    grad_normed2 = summed_up[:, :D] + matmul_back(grad_low2, adapt_up_in)
    norm2_value, norm2_pull = jax.vjp(
        lambda values: layer_norm(values, norm2_gain, norm2_shift), mid
    )
    grad_mid = cotangent + norm2_pull(grad_normed2)[0]
    grad_attn = grad_mid.astype(jnp.bfloat16)
    grad_proj_low = (matmul_back(grad_attn, adapt_proj_out) * own_mask).astype(jnp.bfloat16)
    grad_proj_out_part = matmul_over(proj_low, grad_attn)
    grad_attn_all, grad_proj_small = (
        lax.all_gather(grad_attn, "tensor", axis=0, tiled=True),
        lax.all_gather(grad_proj_low, "tensor", axis=0, tiled=True),
    )
    grad_attended = matmul_back(grad_attn_all, proj_weight) + matmul_back(
        grad_proj_small, adapt_proj_in
    )
    grad_proj_in_part = matmul_over(attended, grad_proj_small)
    grad_attended_seq = jnp.take(grad_attended, order_row, axis=0).astype(jnp.bfloat16)
    normed1_again, low1_again_small = (
        lax.all_gather(normed1, "tensor", axis=0, tiled=True),
        lax.all_gather(low1, "tensor", axis=0, tiled=True),
    )
    qkv_seq = jnp.take(project_qkv(normed1_again, low1_again_small), order_row, axis=0)
    low1_all = low1_again_small
    grad_qkv_seq = attention_backward(qkv_seq, grad_attended_seq, log_totals, lengths_row, seq_len)
    grad_qkv = jnp.take(grad_qkv_seq.astype(jnp.bfloat16), inverse, axis=0)
    grad_qkv_out_part = jnp.einsum(
        "ra,rkc->akc", low1_all, grad_qkv, preferred_element_type=jnp.float32
    )
    rows = grad_qkv
    part = jnp.einsum("rkc,dkc->rd", rows, qkv_joined, preferred_element_type=jnp.float32)
    summed_qkv = lax.psum_scatter(
        jnp.concatenate([part[:, :D], part[:, D:]], 1).astype(jnp.bfloat16),
        "tensor",
        scatter_dimension=0,
        tiled=True,
    ).astype(jnp.float32)
    grad_low1 = (summed_qkv[:, D:] * own_mask).astype(jnp.bfloat16)
    grad_qkv_in_part = matmul_over(normed1, grad_low1)
    grad_normed1 = summed_qkv[:, :D] + matmul_back(grad_low1, adapt_qkv_in)
    norm1_value, norm1_pull = jax.vjp(
        lambda values: layer_norm(values, norm1_gain, norm1_shift), inputs
    )
    grad_input = grad_mid + norm1_pull(grad_normed1)[0]
    wide = lax.psum(
        (grad_qkv_in_part, grad_proj_out_part, grad_up_in_part, grad_down_out_part),
        ("dp", "tensor"),
    )
    narrow = (
        lax.psum(grad_qkv_out_part.astype(jnp.bfloat16), "dp").astype(jnp.float32),
        lax.psum(grad_proj_in_part.astype(jnp.bfloat16), "dp").astype(jnp.float32),
        lax.psum(grad_up_out_part.astype(jnp.bfloat16), "dp").astype(jnp.float32),
        lax.psum(grad_down_in_part.astype(jnp.bfloat16), "dp").astype(jnp.float32),
    )
    return (
        result,
        grad_input,
        wide[0],
        narrow[0],
        narrow[1],
        wide[1],
        wide[2],
        narrow[2],
        narrow[3],
        wide[3],
    )


def solution(mesh):
    in_specs = (
        P(("dp", "tensor"), None),
        P(("dp", "tensor"), None),
        P("dp", None),
        P("dp", None),
        P("dp", None),
        P(),
        P(),
        P(None, None, "tensor"),
        P(None, "tensor"),
        P("tensor", None),
        P(),
        P(),
        P(),
        P(None, "tensor"),
        P("tensor"),
        P("tensor", None),
        P(),
        P(),
        P(None, None, "tensor"),
        P("tensor", None),
        P(),
        P(),
        P(None, "tensor"),
        P("tensor", None),
        P(),
    )
    out_specs = (
        P(("dp", "tensor"), None),
        P(("dp", "tensor"), None),
        P(),
        P(None, None, "tensor"),
        P("tensor", None),
        P(),
        P(),
        P(None, "tensor"),
        P("tensor", None),
        P(),
    )
    return jax.shard_map(body, mesh=mesh, in_specs=in_specs, out_specs=out_specs, check_vma=False)
```

profile of v0, /device:TPU:0, one launch (start us, length us, event | category | flops | bytes accessed | tf_op | source)
XLA Modules:
  0.0 638.7 jit_solution(10005724395536461428)
XLA Ops:
  12.8 4.3 scatter_custom_fusion
  20.2 8.9 %all_gather.29 = bf16[1024,128]{1,0:T(8,128)(2,1)S(1)} all-gather(bf16[256,128]{1,0:T(8,128)(2,1)S(1)} %fusion.97), channel_id=1, replica_groups=mesh['dp'=8,'tensor'=4] {'tensor'}, dimensions={0}, use_global_device_ids=true | all-gather | bytes 327680 | tf_op jit(solution)/shard_map/all_gather | solution.py:197
  31.9 6.9 %all-gather.5.cloned.1.call-done = bf16[1024,1024]{1,0:T(8,128)(2,1)} async-done(((bf16[256,1024]{1,0:T(8,128)(2,1)}), bf16[1024,1024]{1,0:T(8,128)(2,1)}) %all-gather.5.cloned.1.call-update) | async-done | bytes 2097168 | tf_op jit(solution)/shard_map/all_gather | solution.py:196
  38.8 3.8 fusion.84
  43.3 2.7 copy.65
  46.0 10.1 %gather_fusion.2 = bf16[1024,3,256]{2,1,0:T(4,128)(2,1)} fusion(bf16[1024,3,256]{2,1,0:T(4,128)(2,1)} %copy.65, s32[1024]{0:T(1024)S(1)} %fusion.129), kind=kCustom, calls=%fused_computation.clone | custom fusion | bytes 3149824 | tf_op jit(solution)/shard_map/jit(_take)/gather | solution.py:201
  56.1 6.3 broadcast_select_fusion.1
  62.4 2.9 copy.66
  65.3 15.9 %while.32 = (s32[]{:T(128)}, bf16[2,512,256]{1,2,0:T(8,128)(2,1)S(1)}, f32[2,4,512]{2,1,0:T(4,128)S(1)}, bf16[1024,3,4,64]{0,3,2,1:T(8,128)(2,1)S(1)}, s32[2]{0:...) while((s32[]{:T(128)}, ...), condition=%wide.region_7.9_spmd, body=%wide.region_4.8_spmd.sunk | while | flops 281541120 | bytes 18417900 | solution.py:72
  81.4 4.4 gather_fusion
  91.6 32.2 %reduce-scatter.5.cloned.1.call-done = bf16[256,1152]{1,0:T(8,128)(2,1)} async-done(((bf16[1024,1152]{1,0:T(8,128)(2,1)}), bf16[256,1152]{1,0:T(8,128)(2,1)}) %reduce-scatter.5.cloned.1.call-update) | async-done | bytes 589840 | tf_op jit(solution)/shard_map/reduce_scatter | solution.py:207
  129.0 6.4 %all_gather.33 = bf16[1024,128]{1,0:T(8,128)(2,1)} all-gather(bf16[256,128]{1,0:T(8,128)(2,1)S(1)} %fusion.99), channel_id=1, replica_groups=mesh['dp'=8,'tensor'=4] {'tensor'}, dimensions={0}, use_global_device_ids=true | all-gather | bytes 327680 | tf_op jit(solution)/shard_map/all_gather | solution.py:240
  135.4 13.3 %all-gather.9.cloned.1.call-done = bf16[1024,1024]{1,0:T(8,128)(2,1)} async-done(((bf16[256,1024]{1,0:T(8,128)(2,1)}), bf16[1024,1024]{1,0:T(8,128)(2,1)}) %all-gather.9.cloned.1.call-update) | async-done | bytes 2097168 | tf_op jit(solution)/shard_map/all_gather | solution.py:239
  148.7 6.6 %fusion.153 = f32[1024,1024]{1,0:T(8,128)} fusion(bf16[1024,1024]{1,0:T(8,128)(2,1)} %all-gather.9.cloned.1.call-done, bf16[1024,1024]{1,0:T(8,128)(2,1)} %param.46), kind=kOutput, calls=%fused_computation.219 | convolution fusion | flops 2147483648 | bytes 8388608 | tf_op jit(solution)/shard_map/dot_general | solution.py:25
  155.6 5.8 all_gather.31
  161.4 12.0 %all-gather.7.cloned.1.call-done = bf16[1024,1024]{1,0:T(8,128)(2,1)} async-done(((bf16[256,1024]{1,0:T(8,128)(2,1)}), bf16[1024,1024]{1,0:T(8,128)(2,1)}) %all-gather.7.cloned.1.call-update) | async-done | bytes 2097168 | tf_op jit(solution)/shard_map/all_gather | solution.py:218
  173.4 4.6 fusion.152
  181.8 3.2 fusion.76
  186.5 4.2 convolution_convert_fusion
  190.7 33.2 %reduce-scatter.9.cloned.1.call-done = bf16[256,1152]{1,0:T(8,128)(2,1)} async-done(((bf16[1024,1152]{1,0:T(8,128)(2,1)}), bf16[256,1152]{1,0:T(8,128)(2,1)}) %reduce-scatter.9.cloned.1.call-update) | async-done | bytes 589840 | tf_op jit(solution)/shard_map/reduce_scatter | solution.py:258
  229.6 6.5 %fusion.77 = bf16[1024,1152]{1,0:T(8,128)(2,1)S(1)} fusion(bf16[1024,128]{1,0:T(8,128)(2,1)S(1)} %copy-done.64, bf16[1024,1024]{1,0:T(8,128)(2,1)} %param.46, f32[1024,1024]{1,0:T(8,128)} %copy-done.18), kind=kOutput, calls=%fused_computation.87 | convolution fusion | flops 2430074880 | bytes 8912896 | tf_op jit(solution)/shard_map/dot_general | solution.py:21
  240.9 4.8 convolution_convert_fusion.1
  246.1 6.3 all_gather.35
  254.6 2.4 fusion.154
  257.4 5.5 gather_fusion.1
  266.1 62.1 %while.33 = (s32[]{:T(128)}, bf16[2,512,4,64]{1,3,2,0:T(8,128)(2,1)}, bf16[2,512,4,64]{1,3,2,0:T(8,128)(2,1)}, bf16[2,512,4,64]{1,3,2,0:T(8,128)(2,1)}, bf16[102...) while((s32[]{:T(128)}, ...), condition=%wide.region_17.19_spmd, body=%wide.region_15.18_spmd.sunk | while | flops 686298624 | bytes 57437636 | solution.py:112
  271.6 2.8 fusion.230
  274.4 3.3 subtract_exponential_fusion.3
  277.6 7.9 %fusion.232 = bf16[2,512,4,64]{1,3,2,0:T(8,128)(2,1)} fusion(bf16[2,512,4,64]{1,3,2,0:T(8,128)(2,1)} %get-tuple-element.493, s32[]{:T(128)S(6)} %copy.112, f32[4,512,512]{1,2,0:T(8,128)} %subtract_exponential_fusion.3, f32[4,512,512]{1,2,0:T(8,128)} %fusion.230, bf16[1024,1,4,64]{0,3,2,1:T(8,128)(2,1)} %copy-done.5, s32[]{:T(128)S(6)} %select_n.203), kind=kOutput, calls=%fused_computation.43.clone.1 | convolution fusion | flops 139463168 | bytes 17563656 | tf_op jit(solution)/shard_map/while/body/eval_jaxpr/hqk,qhc->khc/dot_general | solution.py:102
  285.6 8.0 %fusion.231 = bf16[2,512,4,64]{1,3,2,0:T(8,128)(2,1)} fusion(bf16[2,512,4,64]{1,3,2,0:T(8,128)(2,1)} %get-tuple-element.492, s32[]{:T(128)S(6)} %copy.112, f32[4,512,512]{1,2,0:T(8,128)} %subtract_exponential_fusion.3, f32[4,512,512]{1,2,0:T(8,128)} %fusion.230, bf16[1024,1,4,64]{0,3,2,1:T(8,128)(2,1)} %copy-done.4, s32[]{:T(128)S(6)} %select_n.203), kind=kOutput, calls=%fused_computation.41.clone.1 | convolution fusion | flops 139463168 | bytes 17563656 | tf_op jit(solution)/shard_map/while/body/eval_jaxpr/hqk,khc->qhc/dot_general | solution.py:101
  293.6 3.7 fusion.233
  302.7 2.8 fusion.230
  305.4 3.3 subtract_exponential_fusion.3
  308.7 7.9 %fusion.232 = bf16[2,512,4,64]{1,3,2,0:T(8,128)(2,1)} fusion(bf16[2,512,4,64]{1,3,2,0:T(8,128)(2,1)} %get-tuple-element.493, s32[]{:T(128)S(6)} %copy.112, f32[4,512,512]{1,2,0:T(8,128)} %subtract_exponential_fusion.3, f32[4,512,512]{1,2,0:T(8,128)} %fusion.230, bf16[1024,1,4,64]{0,3,2,1:T(8,128)(2,1)} %copy-done.5, s32[]{:T(128)S(6)} %select_n.203), kind=kOutput, calls=%fused_computation.43.clone.1 | convolution fusion | flops 139463168 | bytes 17563656 | tf_op jit(solution)/shard_map/while/body/eval_jaxpr/hqk,qhc->khc/dot_general | solution.py:102
  316.6 8.0 %fusion.231 = bf16[2,512,4,64]{1,3,2,0:T(8,128)(2,1)} fusion(bf16[2,512,4,64]{1,3,2,0:T(8,128)(2,1)} %get-tuple-element.492, s32[]{:T(128)S(6)} %copy.112, f32[4,512,512]{1,2,0:T(8,128)} %subtract_exponential_fusion.3, f32[4,512,512]{1,2,0:T(8,128)} %fusion.230, bf16[1024,1,4,64]{0,3,2,1:T(8,128)(2,1)} %copy-done.4, s32[]{:T(128)S(6)} %select_n.203), kind=kOutput, calls=%fused_computation.41.clone.1 | convolution fusion | flops 139463168 | bytes 17563656 | tf_op jit(solution)/shard_map/while/body/eval_jaxpr/hqk,khc->qhc/dot_general | solution.py:101
  324.6 3.7 fusion.233
  328.3 2.4 copy.85
  330.6 3.9 reshape.388
  336.9 4.8 reshape.386
  343.0 4.8 reshape.387
  347.8 5.8 pad_maximum_fusion.2
  353.6 10.2 %gather_fusion.3 = bf16[1024,3,256]{2,1,0:T(4,128)(2,1)} fusion(bf16[1024,3,256]{2,1,0:T(4,128)(2,1)} %pad_maximum_fusion.2, s32[1024]{0:T(1024)S(1)} %copy-done.40), kind=kCustom, calls=%fused_computation.1.clone | custom fusion | bytes 3149824 | tf_op jit(solution)/shard_map/jit(_take)/gather | solution.py:290
  363.8 5.3 broadcast_select_fusion
  371.9 5.7 bitcast_convert_fusion
  383.6 2.3 fusion.95
  386.0 61.0 %all-reduce.7.cloned.1.call-done = (bf16[128,3,256]{2,0,1:T(8,128)(2,1)}, bf16[256,128]{1,0:T(8,128)(2,1)}, bf16[128,1024]{1,0:T(8,128)(2,1)}, bf16[1024,128]{1,0:T(8,128)(2,1)}) async-done(((bf16[128,3,256]{2,0,1:T(8,128)(2,1)}, bf16[256,128]{1,0:T(8,128)(2,1)}, bf16[128,1024]{1,0:T(8,128)(2,1)}, bf16[1024,128]{1,0:T(8,128)(2,1)}), (bf16[128,3,256]{2,0,1:T(8,128)(2,1)}, bf16[256,128]{1,0:T(8,128)(2,1)}, ...) | async-done | bytes 786448 | tf_op jit(solution)/shard_map/psum | solution.py:314
  453.7 27.9 %reduce-scatter.11.cloned.1.call-done = bf16[256,1152]{1,0:T(8,128)(2,1)} async-done(((bf16[1024,1152]{1,0:T(8,128)(2,1)}), bf16[256,1152]{1,0:T(8,128)(2,1)}) %reduce-scatter.11.cloned.1.call-update) | async-done | bytes 589840 | tf_op jit(solution)/shard_map/reduce_scatter | solution.py:296
  489.3 134.8 %all-reduce.5.cloned.1.call-done = (f32[1024,128]{1,0:T(8,128)}, f32[128,1024]{1,0:T(8,128)}, f32[1024,128]{1,0:T(8,128)}, f32[128,1024]{1,0:T(8,128)}) async-done(((f32[1024,128]{1,0:T(8,128)}, f32[128,1024]{1,0:T(8,128)}, f32[1024,128]{1,0:T(8,128)}, f32[128,1024]{1,0:T(8,128)}), (f32[1024,128]{1,0:T(8,128)}, f32[128,1024]{1,0:T(8,128)}, f32[1024,128]{1,0:T(8,128)}, ...) | async-done | bytes 2097168 | tf_op jit(solution)/shard_map/psum | solution.py:309
  (277 shorter events, 95.3 us)
Async XLA Ops:
  7.2 148.1 %copy-start = (bf16[1024,128]{1,0:T(8,128)(2,1)S(1)}, bf16[1024,128]{1,0:T(8,128)(2,1)}, u32[]{:S(2)}) copy-start(bf16[1024,128]{1,0:T(8,128)(2,1)} %param.52) | copy-start | bytes 786436
  7.2 31.6 %all-gather.5.cloned.1.call-start = ((), (), s32[]{:S(2)}) async-start(), calls=%async_computation.4 | async-start | bytes 2621440 | tf_op jit(solution)/shard_map/all_gather | solution.py:196
  8.5 30.4 %copy-start.38 = (f32[256]{0:T(256)}, f32[256]{0:T(256)S(1)}, u32[]{:S(2)}) copy-start(f32[256]{0:T(256)S(1)} %broadcast_multiply_fusion.1) | copy-start | bytes 3076
  9.8 29.0 %copy-start.55 = (f32[256]{0:T(256)}, f32[256]{0:T(256)S(1)}, u32[]{:S(2)}) copy-start(f32[256]{0:T(256)S(1)} %fusion.103) | copy-start | bytes 3076
  9.8 29.0 %copy-start.46 = (f32[256]{0:T(256)}, f32[256]{0:T(256)S(1)}, u32[]{:S(2)}) copy-start(f32[256]{0:T(256)S(1)} %fusion.138) | copy-start | bytes 3076
  12.0 111.8 %reduce-scatter.5.cloned.1.call-start = ((), (), s32[]{:S(2)}) async-start(), calls=%async_computation.5 | async-start | bytes 2949120 | tf_op jit(solution)/shard_map/reduce_scatter | solution.py:207
  17.2 14.0 %copy-start.58 = (s32[128]{0:T(128)}, s32[128]{0:T(128)S(1)}, u32[]{:S(2)}) copy-start(s32[128]{0:T(128)S(1)} %and_select_fusion) | copy-start | bytes 1540
  18.5 24.1 %copy-start.36 = (s32[1024]{0:T(1024)}, s32[1024]{0:T(1024)S(1)}, u32[]{:S(2)}) copy-start(s32[1024]{0:T(1024)S(1)} %fusion.125) | copy-start | bytes 12292
  29.1 13.6 %copy-start.19 = (bf16[1024,128]{1,0:T(8,128)(2,1)}, bf16[1024,128]{1,0:T(8,128)(2,1)S(1)}, u32[]{:S(2)}) copy-start(bf16[1024,128]{1,0:T(8,128)(2,1)S(1)} %all_gather.29) | copy-start | bytes 786436
  31.2 24.9 %copy-start.49 = (pred[1024]{0:T(1024)(128)(4,1)}, pred[1024]{0:T(1024)(128)(4,1)S(1)}, u32[]{:S(2)}) copy-start(pred[1024]{0:T(1024)(128)(4,1)S(1)} %compare_and_fusion) | copy-start | bytes 3076
  31.9 10.8 %copy-start.34 = (bf16[128,3,256]{2,0,1:T(8,128)(2,1)S(1)}, bf16[128,3,256]{2,0,1:T(8,128)(2,1)}, u32[]{:S(2)}) copy-start(bf16[128,3,256]{2,0,1:T(8,128)(2,1)} %param.49) | copy-start | bytes 589828
  56.1 9.2 %copy-start.65 = (s32[1,2]{1,0:T(1,128)S(1)}, s32[1,2]{1,0:T(1,128)}, u32[]{:S(2)}) copy-start(s32[1,2]{1,0:T(1,128)} %param.33) | copy-start | bytes 28
  88.9 34.9 %copy-start.2 = (bf16[256,1024]{1,0:T(8,128)(2,1)S(1)}, bf16[256,1024]{1,0:T(8,128)(2,1)}, u32[]{:S(2)}) copy-start(bf16[256,1024]{1,0:T(8,128)(2,1)} %param.31) | copy-start | bytes 1572868
  90.6 58.1 %all-gather.9.cloned.1.call-start = ((), (), s32[]{:S(2)}) async-start(), calls=%async_computation.8 | async-start | bytes 2621440 | tf_op jit(solution)/shard_map/all_gather | solution.py:239
  91.6 81.8 %all-gather.7.cloned.1.call-start = ((), (), s32[]{:S(2)}) async-start(), calls=%async_computation.6 | async-start | bytes 2621440 | tf_op jit(solution)/shard_map/all_gather | solution.py:218
  127.5 96.4 %reduce-scatter.9.cloned.1.call-start = ((), (), s32[]{:S(2)}) async-start(), calls=%async_computation.9 | async-start | bytes 2949120 | tf_op jit(solution)/shard_map/reduce_scatter | solution.py:258
  135.4 19.9 %copy-start.15 = (bf16[256,1024]{1,0:T(8,128)(2,1)S(1)}, bf16[256,1024]{1,0:T(8,128)(2,1)}, u32[]{:S(2)}) copy-start(bf16[256,1024]{1,0:T(8,128)(2,1)} %add_convert_fusion.1) | copy-start | bytes 1572868
  161.3 16.6 %copy-start.31 = (bf16[128,1024]{1,0:T(8,128)(2,1)S(1)}, bf16[128,1024]{1,0:T(8,128)(2,1)}, u32[]{:S(2)}) copy-start(bf16[128,1024]{1,0:T(8,128)(2,1)} %param.53) | copy-start | bytes 786436
  190.7 35.7 %copy-start.57 = (f32[256]{0:T(256)S(1)}, f32[256]{0:T(256)}, u32[]{:S(2)}) copy-start(f32[256]{0:T(256)} %copy-done.56) | copy-start | bytes 3076
  190.7 35.8 %copy-start.42 = (f32[256]{0:T(256)S(1)}, f32[256]{0:T(256)}, u32[]{:S(2)}) copy-start(f32[256]{0:T(256)} %copy-done.41) | copy-start | bytes 3076
  190.7 35.8 %copy-start.54 = (f32[256]{0:T(256)S(1)}, f32[256]{0:T(256)}, u32[]{:S(2)}) copy-start(f32[256]{0:T(256)} %copy-done.53) | copy-start | bytes 3076
  190.7 63.9 %all-gather.11.cloned.1.call-start = ((), (), s32[]{:S(2)}) async-start(), calls=%async_computation.10 | async-start | bytes 2621440 | tf_op jit(solution)/shard_map/all_gather | solution.py:275
  228.9 150.7 %reduce-scatter.7.cloned.1.call-start = ((), (), s32[]{:S(2)}) async-start(), calls=%async_computation.7 | async-start | bytes 2949120 | tf_op jit(solution)/shard_map/reduce_scatter | solution.py:227
  245.7 201.2 %all-reduce.7.cloned.1.call-start = ((), (), s32[]{:S(2)}) async-start(), calls=%async_computation.13 | async-start | bytes 1572864 | tf_op jit(solution)/shard_map/psum | solution.py:314
  257.3 7.6 %copy-start.50 = (pred[1024]{0:T(1024)(128)(4,1)S(1)}, pred[1024]{0:T(1024)(128)(4,1)}, u32[]{:S(2)}) copy-start(pred[1024]{0:T(1024)(128)(4,1)} %copy-done.49) | copy-start | bytes 3076
  285.6 11.7 %copy-start.67 = (s32[2]{0:T(128)S(1)}, s32[2]{0:T(128)}, u32[]{:S(2)}) copy-start(s32[2]{0:T(128)} %copy-done.66) | copy-start | bytes 28 | tf_op jit(solution)/shard_map/while
  316.6 11.7 %copy-start.67 = (s32[2]{0:T(128)S(1)}, s32[2]{0:T(128)}, u32[]{:S(2)}) copy-start(s32[2]{0:T(128)} %copy-done.66) | copy-start | bytes 28 | tf_op jit(solution)/shard_map/while
  328.3 13.4 %copy-start.30 = (bf16[2,512,4,64]{1,3,2,0:T(8,128)(2,1)S(1)}, bf16[2,512,4,64]{1,3,2,0:T(8,128)(2,1)}, u32[]{:S(2)}) copy-start(bf16[2,512,4,64]{1,3,2,0:T(8,128)(2,1)} %get-tuple-element.261) | copy-start | bytes 1572868
  341.6 12.0 %copy-start.40 = (s32[1024]{0:T(1024)S(1)}, s32[1024]{0:T(1024)}, u32[]{:S(2)}) copy-start(s32[1024]{0:T(1024)} %get-tuple-element.326) | copy-start | bytes 12292
  347.8 16.0 %copy-start.48 = (pred[1024]{0:T(1024)(128)(4,1)S(1)}, pred[1024]{0:T(1024)(128)(4,1)}, u32[]{:S(2)}) copy-start(pred[1024]{0:T(1024)(128)(4,1)} %compare_and_fusion.1) | copy-start | bytes 3076
  353.6 16.8 %copy-start.20 = (bf16[1024,128]{1,0:T(8,128)(2,1)S(1)}, bf16[1024,128]{1,0:T(8,128)(2,1)}, u32[]{:S(2)}) copy-start(bf16[1024,128]{1,0:T(8,128)(2,1)} %copy-done.19) | copy-start | bytes 786436
  363.8 8.1 %copy-start.35 = (bf16[128,3,256]{2,0,1:T(8,128)(2,1)S(1)}, bf16[128,3,256]{2,0,1:T(8,128)(2,1)}, u32[]{:S(2)}) copy-start(bf16[128,3,256]{2,0,1:T(8,128)(2,1)} %param.49) | copy-start | bytes 589828
  371.5 6.1 copy-start.13
  371.6 8.1 %copy-start.11 = (bf16[256,1024]{1,0:T(8,128)(2,1)S(1)}, bf16[256,1024]{1,0:T(8,128)(2,1)}, u32[]{:S(2)}) copy-start(bf16[256,1024]{1,0:T(8,128)(2,1)} %convert_element_type.131) | copy-start | bytes 1572868
  371.6 110.1 %reduce-scatter.11.cloned.1.call-start = ((), (), s32[]{:S(2)}) async-start(), calls=%async_computation.11 | async-start | bytes 2949120 | tf_op jit(solution)/shard_map/reduce_scatter | solution.py:296
  377.6 6.0 copy-start.27
  377.6 6.0 copy-start.61
  377.6 246.5 %all-reduce.5.cloned.1.call-start = ((), (), s32[]{:S(2)}) async-start(), calls=%async_computation.12 | async-start | bytes 4194304 | tf_op jit(solution)/shard_map/psum | solution.py:309
  379.6 104.2 %copy-start.14 = (bf16[256,1024]{1,0:T(8,128)(2,1)S(1)}, bf16[256,1024]{1,0:T(8,128)(2,1)}, u32[]{:S(2)}) copy-start(bf16[256,1024]{1,0:T(8,128)(2,1)} %fusion.106) | copy-start | bytes 1572868
  386.0 99.1 %copy-start.3 = (bf16[256,1024]{1,0:T(8,128)(2,1)S(1)}, bf16[256,1024]{1,0:T(8,128)(2,1)}, u32[]{:S(2)}) copy-start(bf16[256,1024]{1,0:T(8,128)(2,1)} %param.31) | copy-start | bytes 1572868
  386.0 99.1 %copy-start.28 = (bf16[1024,128]{1,0:T(8,128)(2,1)S(1)}, bf16[1024,128]{1,0:T(8,128)(2,1)}, u32[]{:S(2)}) copy-start(bf16[1024,128]{1,0:T(8,128)(2,1)} %param.48) | copy-start | bytes 786436
  386.0 99.1 %copy-start.39 = (f32[256]{0:T(256)S(1)}, f32[256]{0:T(256)}, u32[]{:S(2)}) copy-start(f32[256]{0:T(256)} %copy-done.38) | copy-start | bytes 3076
  386.0 99.1 %copy-start.43 = (f32[1024]{0:T(1024)S(1)}, f32[1024]{0:T(1024)}, u32[]{:S(2)}) copy-start(f32[1024]{0:T(1024)} %param.36) | copy-start | bytes 12292
  450.2 37.3 %copy-start.47 = (f32[256]{0:T(256)S(1)}, f32[256]{0:T(256)}, u32[]{:S(2)}) copy-start(f32[256]{0:T(256)} %copy-done.46) | copy-start | bytes 3076
  453.7 34.1 %copy-start.8 = (f32[256,1024]{1,0:T(8,128)S(1)}, f32[256,1024]{1,0:T(8,128)}, u32[]{:S(2)}) copy-start(f32[256,1024]{1,0:T(8,128)} %param.32) | copy-start | bytes 3145732
  453.7 34.1 %copy-start.10 = (f32[256,1024]{1,0:T(8,128)S(1)}, f32[256,1024]{1,0:T(8,128)}, u32[]{:S(2)}) copy-start(f32[256,1024]{1,0:T(8,128)} %copy-done.9) | copy-start | bytes 3145732
  453.7 34.1 %copy-start.52 = (f32[256]{0:T(256)S(1)}, f32[256]{0:T(256)}, u32[]{:S(2)}) copy-start(f32[256]{0:T(256)} %copy-done.51) | copy-start | bytes 3076
  487.8 143.8 %copy-start.1 = (bf16[1024,128]{1,0:T(8,128)(2,1)S(1)}, bf16[1024,128]{1,0:T(8,128)(2,1)}, u32[]{:S(2)}) copy-start(bf16[1024,128]{1,0:T(8,128)(2,1)} %param.52) | copy-start | bytes 786436
  (35 other events, 100.8 us)
Sparse Core Ops, SparseCore 0:
  12.1 26.6 all-gather.4
  90.7 33.0 reduce-scatter.4
  126.0 22.5 all-gather.8
  150.7 22.5 all-gather.6
  190.8 33.0 reduce-scatter.8
  229.0 23.5 all-gather.10
  255.1 33.1 reduce-scatter.6
  371.7 75.2 all-reduce.6
  449.5 32.0 reduce-scatter.10
  489.2 134.8 all-reduce.4
where the time goes:
time: 643 us; the launch traced here: 639 us
  waiting for transfers between devices  321 us (50%)
  matrix products  123 us (19%)
  local copies, waits for them, and re-layouts  87.2 us (14%)
  other arithmetic  53.3 us (8%)
  blocking collectives  27.4 us (4%)
  between operations  15.3 us (2%)
  loops' own time  10.6 us (2%)
    psum x1, waiting for transfers between devices, body(): lax.psum((grad_qkv_in_part, grad_proj_out_part, grad_up_in_part, grad_dow...  135 us
    reduce_scatter x2, waiting for transfers between devices, body(): lax.psum_scatter(jnp.concatenate([part[:, :D], part[:, D:]], 1).astype(jn...  61 us
    psum x1, waiting for transfers between devices, body(): lax.psum(grad_qkv_out_part.astype(jnp.bfloat16), 'dp').astype(jnp.float32)  61 us
    reduce_scatter x2, waiting for transfers between devices, body(): lax.psum_scatter(jnp.concatenate([part[:, :D], part[:, D:] * mask_rows],...  32.2 us
    dot_general x9, matrix products, matmul_back(): lax.dot_general(left, right, (((1,), (1,)), ((), ())), preferred_element_...  21.5 us
    another operation x6, local copies, waits for them, and re-layouts, attention_backward(): return jnp.stack([grad_query, grad_key, grad_value], 1)  19.6 us
    dot_general x8, matrix products, matmul(): return jnp.dot(left, right, preferred_element_type=jnp.float32)  19.2 us
    unnamed x134, local copies, waits for them, and re-layouts  17.1 us
  transfers between devices with their start and end apart: 10, of which 8 were waited for; matrix products, arithmetic and copies ran while one was open for 28% of the time, Pallas kernels for 0%

commit v1 on v0

--- a/solution.py
+++ b/solution.py
@@ -1,3 +1,4 @@
+import functools
 import math
 import jax
 import jax.numpy as jnp
@@ -9,6 +10,32 @@
 RANK = 16
 EPSILON = 1e-05
 NEGATIVE = -1000000000.0
+
+
+def _end_sums_all(load, ax_name):
+    newest, tile_out, reached = (lax.axis_size(ax_name), lax.axis_index(ax_name), load.shape[0])
+    buffer = [(num, (num + 1) % newest) for num in range(newest)]
+    samples = [(num, (num - 1) % newest) for num in range(newest)]
+    response = jnp.zeros((*load.shape[:0], newest * reached, *load.shape[1:]), load.dtype)
+    response = lax.dynamic_update_slice_in_dim(response, load, tile_out * reached, axis=0)
+    outer = fresh = load
+    u_next = newest // 2
+    no = 1
+    while no < u_next + 1:
+        outer = lax.ppermute(outer, ax_name, buffer)
+        response = lax.dynamic_update_slice_in_dim(
+            response, outer, (tile_out - no) % newest * reached, axis=0
+        )
+        if no < newest - u_next:
+            fresh = lax.ppermute(fresh, ax_name, samples)
+            response = lax.dynamic_update_slice_in_dim(
+                response, fresh, (tile_out + no) % newest * reached, axis=0
+            )
+        no += 1
+    return response
+
+
+lift_packet_on_mesh = functools.partial(_end_sums_all, ax_name="tensor")
 
 
 def layer_norm(values, gain, shift):
@@ -236,7 +263,7 @@
     grad_down_low = (matmul_back(grad_mlp, adapt_down_out) * own_mask).astype(jnp.bfloat16)
     grad_down_out_part = matmul_over(down_low, grad_mlp)
     grad_mlp_all, grad_down_small = (
-        lax.all_gather(grad_mlp, "tensor", axis=0, tiled=True),
+        lift_packet_on_mesh(grad_mlp),
         lax.all_gather(grad_down_low, "tensor", axis=0, tiled=True),
     )
     normed2_again, low2_again_small = (

time: 643 us -> 646 us (level)
  waiting for transfers between devices: 321 us -> 301 us
  blocking collectives: 27.4 us -> 45.1 us
    all_gather x1, blocking collectives: 6.41 us -> 24 us  [body(): lax.all_gather(grad_down_low, 'tensor', axis=0, tiled=True)]
    all_gather x1 -> x0, waiting for transfers between devices: 13.3 us -> none  [body(): lax.all_gather(grad_mlp, 'tensor', axis=0, tiled=True)]
    all_gather x1, waiting for transfers between devices: 12 us -> 0.01 us  [body(): lax.all_gather(normed2, 'tensor', axis=0, tiled=True)]
    unnamed x134 -> x150, local copies, waits for them, and re-layouts: 17.1 us -> 16.1 us
  transfers between devices with their start and end apart: 10 -> 12, of which waited for: 8 -> 7; matrix products, arithmetic and copies ran while one was open for 28% -> 27% of each run, Pallas kernels for 0% -> 0%
where the time goes in v1:
time: 646 us; the launch traced here: 642 us
  waiting for transfers between devices  301 us (47%)
  matrix products  124 us (19%)
  local copies, waits for them, and re-layouts  90.6 us (14%)
  other arithmetic  52.5 us (8%)
  blocking collectives  45.1 us (7%)
  between operations  15.1 us (2%)
  loops' own time  10.6 us (2%)
    psum x1, waiting for transfers between devices, body(): lax.psum((grad_qkv_in_part, grad_proj_out_part, grad_up_in_part, grad_dow...  135 us
    reduce_scatter x2, waiting for transfers between devices, body(): lax.psum_scatter(jnp.concatenate([part[:, :D], part[:, D:]], 1).astype(jn...  61.8 us
    psum x1, waiting for transfers between devices, body(): lax.psum(grad_qkv_out_part.astype(jnp.bfloat16), 'dp').astype(jnp.float32)  60.9 us
    reduce_scatter x2, waiting for transfers between devices, body(): lax.psum_scatter(jnp.concatenate([part[:, :D], part[:, D:] * mask_rows],...  33.2 us
    all_gather x1, blocking collectives, body(): lax.all_gather(grad_down_low, 'tensor', axis=0, tiled=True)  24 us
    dot_general x9, matrix products, matmul_back(): lax.dot_general(left, right, (((1,), (1,)), ((), ())), preferred_element_...  22.7 us
    dot_general x8, matrix products, matmul(): return jnp.dot(left, right, preferred_element_type=jnp.float32)  19.3 us
    another operation x6, local copies, waits for them, and re-layouts, attention_backward(): return jnp.stack([grad_query, grad_key, grad_value], 1)  18.7 us
  transfers between devices with their start and end apart: 12, of which 7 were waited for; matrix products, arithmetic and copies ran while one was open for 27% of the time, Pallas kernels for 0%

profile of v1, /device:TPU:0, one launch (start us, length us, event | category | flops | bytes accessed | tf_op | source)
XLA Modules:
  0.0 641.6 jit_solution(13292792012993617924)
XLA Ops:
  13.0 4.3 scatter_custom_fusion
  20.6 9.1 %all_gather.26 = bf16[1024,128]{1,0:T(8,128)(2,1)S(1)} all-gather(bf16[256,128]{1,0:T(8,128)(2,1)S(1)} %fusion.97), channel_id=1, replica_groups=mesh['dp'=8,'tensor'=4] {'tensor'}, dimensions={0}, use_global_device_ids=true | all-gather | bytes 327680 | tf_op jit(solution)/shard_map/all_gather | solution.py:224
  30.5 8.5 %all-gather.4.cloned.1.call-done = bf16[1024,1024]{1,0:T(8,128)(2,1)} async-done(((bf16[256,1024]{1,0:T(8,128)(2,1)}), bf16[1024,1024]{1,0:T(8,128)(2,1)}) %all-gather.4.cloned.1.call-update) | async-done | bytes 2097168 | tf_op jit(solution)/shard_map/all_gather | solution.py:223
  39.0 3.4 fusion.84
  44.3 8.7 %gather_fusion.2 = bf16[1024,3,256]{2,1,0:T(4,128)(2,1)} fusion(bf16[1024,3,256]{2,1,0:T(4,128)(2,1)S(1)} %copy.65, s32[1024]{0:T(1024)S(1)} %fusion.129), kind=kCustom, calls=%fused_computation.clone | custom fusion | bytes 3149824 | tf_op jit(solution)/shard_map/jit(_take)/gather | solution.py:228
  53.0 6.3 broadcast_select_fusion.1
  59.3 2.9 copy.66
  62.2 17.3 %while.32 = (s32[]{:T(128)}, bf16[2,512,256]{1,2,0:T(8,128)(2,1)}, f32[2,4,512]{2,1,0:T(4,128)S(1)}, bf16[1024,3,4,64]{0,3,2,1:T(8,128)(2,1)S(1)}, s32[2]{0:T(12...) while((s32[]{:T(128)}, bf16[2,512,256]{1,2,0:T(8,128)(2,1)}, ...), condition=%wide.region_7.9_spmd, body=%wide.region_4.8_spmd.sunk | while | flops 281541120 | bytes 18417900 | solution.py:99
  80.8 4.4 gather_fusion
  89.4 33.2 %reduce-scatter.5.cloned.1.call-done = bf16[256,1152]{1,0:T(8,128)(2,1)} async-done(((bf16[1024,1152]{1,0:T(8,128)(2,1)}), bf16[256,1152]{1,0:T(8,128)(2,1)}) %reduce-scatter.5.cloned.1.call-update) | async-done | bytes 589840 | tf_op jit(solution)/shard_map/reduce_scatter | solution.py:234
  128.0 2.3 constant_dynamic-update-slice_fusion.4
  133.5 24.0 %all_gather.29 = bf16[1024,128]{1,0:T(8,128)(2,1)S(1)} all-gather(bf16[256,128]{1,0:T(8,128)(2,1)S(1)} %fusion.99), channel_id=1, replica_groups=mesh['dp'=8,'tensor'=4] {'tensor'}, dimensions={0}, use_global_device_ids=true | all-gather | bytes 327680 | tf_op jit(solution)/shard_map/all_gather | solution.py:267
  157.9 3.7 fusion.153
  167.5 5.8 all_gather.28
  173.3 4.6 fusion.152
  180.8 8.1 %fusion.76 = bf16[1024,1024]{1,0:T(8,128)(2,1)S(1)} fusion(f32[1024,1024]{1,0:T(8,128)S(1)} %add_add_fusion, f32[1024,1024]{1,0:T(8,128)S(1)} %copy-done.16, bf16[1024,1024]{1,0:T(8,128)(2,1)} %constant_dynamic-update-slice_fusion.1, bf16[1024,1024]{1,0:T(8,128)(2,1)S(1)} %copy-done.72), kind=kOutput, calls=%fused_computation.79 | convolution fusion | flops 2169503744 | bytes 14680064 | tf_op jit(solution)/shard_map/dot_general | solution.py:52
  190.3 4.2 convolution_convert_fusion
  194.6 34.0 %reduce-scatter.9.cloned.1.call-done = bf16[256,1152]{1,0:T(8,128)(2,1)} async-done(((bf16[1024,1152]{1,0:T(8,128)(2,1)}), bf16[256,1152]{1,0:T(8,128)(2,1)}) %reduce-scatter.9.cloned.1.call-update) | async-done | bytes 589840 | tf_op jit(solution)/shard_map/reduce_scatter | solution.py:285
  233.9 6.5 %fusion.77 = bf16[1024,1152]{1,0:T(8,128)(2,1)S(1)} fusion(bf16[1024,128]{1,0:T(8,128)(2,1)S(1)} %copy-done.35, bf16[1024,1024]{1,0:T(8,128)(2,1)} %param.46, f32[1024,1024]{1,0:T(8,128)} %copy-done.17), kind=kOutput, calls=%fused_computation.87 | convolution fusion | flops 2430074880 | bytes 8912896 | tf_op jit(solution)/shard_map/dot_general | solution.py:48
  245.2 4.8 convolution_convert_fusion.1
  250.4 6.3 all_gather.31
  256.7 2.2 convolution_convert_fusion.4
  258.9 2.4 fusion.154
  261.7 5.5 gather_fusion.1
  270.5 62.6 %while.33 = (s32[]{:T(128)}, bf16[2,512,4,64]{1,3,2,0:T(8,128)(2,1)}, bf16[2,512,4,64]{1,3,2,0:T(8,128)(2,1)}, bf16[2,512,4,64]{1,3,2,0:T(8,128)(2,1)}, bf16[102...) while((s32[]{:T(128)}, ...), condition=%wide.region_17.19_spmd, body=%wide.region_15.18_spmd.sunk | while | flops 686298624 | bytes 57437636 | solution.py:139
  276.0 2.8 fusion.230
  278.7 3.3 subtract_exponential_fusion.3
  282.0 8.0 %fusion.232 = bf16[2,512,4,64]{1,3,2,0:T(8,128)(2,1)} fusion(bf16[2,512,4,64]{1,3,2,0:T(8,128)(2,1)} %get-tuple-element.495, s32[]{:T(128)S(6)} %copy.116, f32[4,512,512]{1,2,0:T(8,128)} %subtract_exponential_fusion.3, f32[4,512,512]{1,2,0:T(8,128)} %fusion.230, bf16[1024,1,4,64]{0,3,2,1:T(8,128)(2,1)} %copy-done.5, s32[]{:T(128)S(6)} %select_n.231), kind=kOutput, calls=%fused_computation.43.clone.1 | convolution fusion | flops 139463168 | bytes 17563656 | tf_op jit(solution)/shard_map/while/body/eval_jaxpr/hqk,qhc->khc/dot_general | solution.py:129
  290.0 8.2 %fusion.231 = bf16[2,512,4,64]{1,3,2,0:T(8,128)(2,1)} fusion(bf16[2,512,4,64]{1,3,2,0:T(8,128)(2,1)} %get-tuple-element.494, s32[]{:T(128)S(6)} %copy.116, f32[4,512,512]{1,2,0:T(8,128)} %subtract_exponential_fusion.3, f32[4,512,512]{1,2,0:T(8,128)} %fusion.230, bf16[1024,1,4,64]{0,3,2,1:T(8,128)(2,1)} %copy-done.4, s32[]{:T(128)S(6)} %select_n.231), kind=kOutput, calls=%fused_computation.41.clone.1 | convolution fusion | flops 139463168 | bytes 17563656 | tf_op jit(solution)/shard_map/while/body/eval_jaxpr/hqk,khc->qhc/dot_general | solution.py:128
  298.2 3.7 fusion.233
  307.3 2.8 fusion.230
  310.1 3.3 subtract_exponential_fusion.3
  313.4 8.0 %fusion.232 = bf16[2,512,4,64]{1,3,2,0:T(8,128)(2,1)} fusion(bf16[2,512,4,64]{1,3,2,0:T(8,128)(2,1)} %get-tuple-element.495, s32[]{:T(128)S(6)} %copy.116, f32[4,512,512]{1,2,0:T(8,128)} %subtract_exponential_fusion.3, f32[4,512,512]{1,2,0:T(8,128)} %fusion.230, bf16[1024,1,4,64]{0,3,2,1:T(8,128)(2,1)} %copy-done.5, s32[]{:T(128)S(6)} %select_n.231), kind=kOutput, calls=%fused_computation.43.clone.1 | convolution fusion | flops 139463168 | bytes 17563656 | tf_op jit(solution)/shard_map/while/body/eval_jaxpr/hqk,qhc->khc/dot_general | solution.py:129
  321.3 8.1 %fusion.231 = bf16[2,512,4,64]{1,3,2,0:T(8,128)(2,1)} fusion(bf16[2,512,4,64]{1,3,2,0:T(8,128)(2,1)} %get-tuple-element.494, s32[]{:T(128)S(6)} %copy.116, f32[4,512,512]{1,2,0:T(8,128)} %subtract_exponential_fusion.3, f32[4,512,512]{1,2,0:T(8,128)} %fusion.230, bf16[1024,1,4,64]{0,3,2,1:T(8,128)(2,1)} %copy-done.4, s32[]{:T(128)S(6)} %select_n.231), kind=kOutput, calls=%fused_computation.41.clone.1 | convolution fusion | flops 139463168 | bytes 17563656 | tf_op jit(solution)/shard_map/while/body/eval_jaxpr/hqk,khc->qhc/dot_general | solution.py:128
  329.5 3.7 fusion.233
  333.1 2.4 copy.85
  335.5 4.0 reshape.388
  340.9 4.8 reshape.386
  347.1 4.8 reshape.387
  351.9 5.8 pad_maximum_fusion.2
  357.7 10.1 %gather_fusion.3 = bf16[1024,3,256]{2,1,0:T(4,128)(2,1)} fusion(bf16[1024,3,256]{2,1,0:T(4,128)(2,1)} %pad_maximum_fusion.2, s32[1024]{0:T(1024)S(1)} %copy-done.45), kind=kCustom, calls=%fused_computation.1.clone | custom fusion | bytes 3149824 | tf_op jit(solution)/shard_map/jit(_take)/gather | solution.py:317
  367.9 5.5 broadcast_select_fusion
  376.0 5.7 bitcast_convert_fusion
  383.8 2.1 fusion.119
  388.0 2.4 fusion.95
  390.4 60.9 %all-reduce.7.cloned.1.call-done = (bf16[128,3,256]{2,0,1:T(8,128)(2,1)}, bf16[256,128]{1,0:T(8,128)(2,1)}, bf16[128,1024]{1,0:T(8,128)(2,1)}, bf16[1024,128]{1,0:T(8,128)(2,1)}) async-done(((bf16[128,3,256]{2,0,1:T(8,128)(2,1)}, bf16[256,128]{1,0:T(8,128)(2,1)}, bf16[128,1024]{1,0:T(8,128)(2,1)}, bf16[1024,128]{1,0:T(8,128)(2,1)}), (bf16[128,3,256]{2,0,1:T(8,128)(2,1)}, bf16[256,128]{1,0:T(8,128)(2,1)}, ...) | async-done | bytes 786448 | tf_op jit(solution)/shard_map/psum | solution.py:341
  458.2 27.8 %reduce-scatter.11.cloned.1.call-done = bf16[256,1152]{1,0:T(8,128)(2,1)} async-done(((bf16[1024,1152]{1,0:T(8,128)(2,1)}), bf16[256,1152]{1,0:T(8,128)(2,1)}) %reduce-scatter.11.cloned.1.call-update) | async-done | bytes 589840 | tf_op jit(solution)/shard_map/reduce_scatter | solution.py:323
  493.2 135.2 %all-reduce.5.cloned.1.call-done = (f32[1024,128]{1,0:T(8,128)}, f32[128,1024]{1,0:T(8,128)}, f32[1024,128]{1,0:T(8,128)}, f32[128,1024]{1,0:T(8,128)}) async-done(((f32[1024,128]{1,0:T(8,128)}, f32[128,1024]{1,0:T(8,128)}, f32[1024,128]{1,0:T(8,128)}, f32[128,1024]{1,0:T(8,128)}), (f32[1024,128]{1,0:T(8,128)}, f32[128,1024]{1,0:T(8,128)}, f32[1024,128]{1,0:T(8,128)}, ...) | async-done | bytes 2097168 | tf_op jit(solution)/shard_map/psum | solution.py:336
  (300 shorter events, 97.4 us)
Async XLA Ops:
  7.2 160.0 %copy-start = (bf16[1024,128]{1,0:T(8,128)(2,1)S(1)}, bf16[1024,128]{1,0:T(8,128)(2,1)}, u32[]{:S(2)}) copy-start(bf16[1024,128]{1,0:T(8,128)(2,1)} %param.52) | copy-start | bytes 786436
  7.2 23.2 %copy-start.42 = (s32[1,1024]{1,0:T(1,128)S(1)}, s32[1,1024]{1,0:T(1,128)}, u32[]{:S(2)}) copy-start(s32[1,1024]{1,0:T(1,128)} %param.34) | copy-start | bytes 12292
  7.2 22.5 %copy-start.70 = (f32[2,256]{1,0:T(2,128)S(1)}, f32[2,256]{1,0:T(2,128)}, u32[]{:S(2)}) copy-start(f32[2,256]{1,0:T(2,128)} %param.39) | copy-start | bytes 6148
  7.2 31.7 %copy-start.73 = (bf16[1024,3,256]{2,0,1:T(8,128)(2,1)S(1)}, bf16[1024,3,256]{2,0,1:T(8,128)(2,1)}, u32[]{:S(2)}) copy-start(bf16[1024,3,256]{2,0,1:T(8,128)(2,1)} %param.38) | copy-start | bytes 4718596
  7.2 31.7 %all-gather.4.cloned.1.call-start = ((), (), s32[]{:S(2)}) async-start(), calls=%async_computation.4 | async-start | bytes 2621440 | tf_op jit(solution)/shard_map/all_gather | solution.py:223
  8.6 9.3 %copy-start.43 = (f32[256]{0:T(256)}, f32[256]{0:T(256)S(1)}, u32[]{:S(2)}) copy-start(f32[256]{0:T(256)S(1)} %broadcast_multiply_fusion.1) | copy-start | bytes 3076
  9.9 8.9 %copy-start.61 = (f32[256]{0:T(256)}, f32[256]{0:T(256)S(1)}, u32[]{:S(2)}) copy-start(f32[256]{0:T(256)S(1)} %fusion.103) | copy-start | bytes 3076
  10.0 8.9 %copy-start.52 = (f32[256]{0:T(256)}, f32[256]{0:T(256)S(1)}, u32[]{:S(2)}) copy-start(f32[256]{0:T(256)S(1)} %fusion.138) | copy-start | bytes 3076
  12.1 110.5 %reduce-scatter.5.cloned.1.call-start = ((), (), s32[]{:S(2)}) async-start(), calls=%async_computation.5 | async-start | bytes 2949120 | tf_op jit(solution)/shard_map/reduce_scatter | solution.py:234
  17.3 13.1 %copy-start.65 = (s32[128]{0:T(128)}, s32[128]{0:T(128)S(1)}, u32[]{:S(2)}) copy-start(s32[128]{0:T(128)S(1)} %and_select_fusion) | copy-start | bytes 1540
  29.7 12.6 %copy-start.18 = (bf16[1024,128]{1,0:T(8,128)(2,1)}, bf16[1024,128]{1,0:T(8,128)(2,1)S(1)}, u32[]{:S(2)}) copy-start(bf16[1024,128]{1,0:T(8,128)(2,1)S(1)} %all_gather.26) | copy-start | bytes 786436
  30.4 22.5 %copy-start.55 = (pred[1024]{0:T(1024)(128)(4,1)}, pred[1024]{0:T(1024)(128)(4,1)S(1)}, u32[]{:S(2)}) copy-start(pred[1024]{0:T(1024)(128)(4,1)S(1)} %compare_and_fusion) | copy-start | bytes 3076
  30.4 11.9 %copy-start.37 = (bf16[128,3,256]{2,0,1:T(8,128)(2,1)S(1)}, bf16[128,3,256]{2,0,1:T(8,128)(2,1)}, u32[]{:S(2)}) copy-start(bf16[128,3,256]{2,0,1:T(8,128)(2,1)} %param.49) | copy-start | bytes 589828
  53.0 9.2 %copy-start.74 = (s32[1,2]{1,0:T(1,128)S(1)}, s32[1,2]{1,0:T(1,128)}, u32[]{:S(2)}) copy-start(s32[1,2]{1,0:T(1,128)} %param.33) | copy-start | bytes 28
  87.7 34.9 %copy-start.2 = (bf16[256,1024]{1,0:T(8,128)(2,1)S(1)}, bf16[256,1024]{1,0:T(8,128)(2,1)}, u32[]{:S(2)}) copy-start(bf16[256,1024]{1,0:T(8,128)(2,1)} %param.31) | copy-start | bytes 1572868
  89.4 83.9 %all-gather.6.cloned.1.call-start = ((), (), s32[]{:S(2)}) async-start(), calls=%async_computation.6 | async-start | bytes 2621440 | tf_op jit(solution)/shard_map/all_gather | solution.py:245
  124.5 7.7 %copy-start.26 = (bf16[128,1024]{1,0:T(8,128)(2,1)S(1)}, bf16[128,1024]{1,0:T(8,128)(2,1)}, u32[]{:S(2)}) copy-start(bf16[128,1024]{1,0:T(8,128)(2,1)} %param.55) | copy-start | bytes 786436
  126.3 102.2 %reduce-scatter.9.cloned.1.call-start = ((), (), s32[]{:S(2)}) async-start(), calls=%async_computation.8 | async-start | bytes 2949120 | tf_op jit(solution)/shard_map/reduce_scatter | solution.py:285
  130.3 27.2 %collective-permute-start = (bf16[256,1024]{1,0:T(8,128)(2,1)}, bf16[256,1024]{1,0:T(8,128)(2,1)}, u32[]{:S(2)}, u32[]{:S(2)}) collective-permute-start(bf16[256,1024]{1,0:T(8,128)(2,1)} %get-tuple-element.319), channel_id=1, source_target_pairs={{0,1},{1,2},{2,3},{3,0},{4,5},{5,6},{6,7},{7,4},{8,9},{9,10},{10,1... | collective-permute-start | bytes 1572872 | tf_op jit(solution)/shard_map/ppermute | solution.py:25
  130.4 33.1 %collective-permute-start.1 = (bf16[256,1024]{1,0:T(8,128)(2,1)}, bf16[256,1024]{1,0:T(8,128)(2,1)}, u32[]{:S(2)}, u32[]{:S(2)}) collective-permute-start(bf16[256,1024]{1,0:T(8,128)(2,1)} %get-tuple-element.319), channel_id=1, source_target_pairs={{0,3},{1,0},{2,1},{3,2},{4,7},{5,4},{6,5},{7,6},{8,11},{9,8},{10,9... | collective-permute-start | bytes 1572872 | tf_op jit(solution)/shard_map/ppermute | solution.py:30
  157.5 7.9 %copy-start.28 = (bf16[1024,128]{1,0:T(8,128)(2,1)}, bf16[1024,128]{1,0:T(8,128)(2,1)S(1)}, u32[]{:S(2)}) copy-start(bf16[1024,128]{1,0:T(8,128)(2,1)S(1)} %all_gather.29) | copy-start | bytes 786436
  157.5 9.7 %copy-start.13 = (bf16[256,1024]{1,0:T(8,128)(2,1)S(1)}, bf16[256,1024]{1,0:T(8,128)(2,1)}, u32[]{:S(2)}) copy-start(bf16[256,1024]{1,0:T(8,128)(2,1)} %add_convert_fusion.1) | copy-start | bytes 1572868
  157.5 8.8 %collective-permute-start.2 = (bf16[256,1024]{1,0:T(8,128)(2,1)}, bf16[256,1024]{1,0:T(8,128)(2,1)S(1)}, u32[]{:S(2)}, u32[]{:S(2)}) collective-permute-start(bf16[256,1024]{1,0:T(8,128)(2,1)} %collective-permute-done), channel_id=1, source_target_pairs={{0,1},{1,2},{2,3},{3,0},{4,5},{5,6},{6,7},{7,4},{8,9},{9,10},{10,1... | collective-permute-start | bytes 1572872 | tf_op jit(solution)/shard_map/ppermute | solution.py:25
  180.8 8.1 %copy-start.17 = (f32[1024,1024]{1,0:T(8,128)}, f32[1024,1024]{1,0:T(8,128)S(1)}, u32[]{:S(2)}) copy-start(f32[1024,1024]{1,0:T(8,128)S(1)} %add_add_fusion) | copy-start | bytes 12582916
  180.8 9.5 %copy-start.71 = (bf16[1024,1024]{1,0:T(8,128)(2,1)S(1)}, bf16[1024,1024]{1,0:T(8,128)(2,1)}, u32[]{:S(2)}) copy-start(bf16[1024,1024]{1,0:T(8,128)(2,1)} %param.44) | copy-start | bytes 6291460
  194.5 35.2 %copy-start.47 = (f32[256]{0:T(256)S(1)}, f32[256]{0:T(256)}, u32[]{:S(2)}) copy-start(f32[256]{0:T(256)} %copy-done.46) | copy-start | bytes 3076
  194.5 35.2 %copy-start.48 = (f32[1024]{0:T(1024)S(1)}, f32[1024]{0:T(1024)}, u32[]{:S(2)}) copy-start(f32[1024]{0:T(1024)} %param.42) | copy-start | bytes 12292
  194.5 35.7 %copy-start.64 = (f32[256]{0:T(256)S(1)}, f32[256]{0:T(256)}, u32[]{:S(2)}) copy-start(f32[256]{0:T(256)} %copy-done.63) | copy-start | bytes 3076
  194.5 36.3 %copy-start.60 = (f32[256]{0:T(256)S(1)}, f32[256]{0:T(256)}, u32[]{:S(2)}) copy-start(f32[256]{0:T(256)} %copy-done.59) | copy-start | bytes 3076
  194.5 64.4 %all-gather.8.cloned.1.call-start = ((), (), s32[]{:S(2)}) async-start(), calls=%async_computation.9 | async-start | bytes 2621440 | tf_op jit(solution)/shard_map/all_gather | solution.py:302
  233.2 150.5 %reduce-scatter.7.cloned.1.call-start = ((), (), s32[]{:S(2)}) async-start(), calls=%async_computation.7 | async-start | bytes 2949120 | tf_op jit(solution)/shard_map/reduce_scatter | solution.py:254
  250.0 201.3 %all-reduce.7.cloned.1.call-start = ((), (), s32[]{:S(2)}) async-start(), calls=%async_computation.12 | async-start | bytes 1572864 | tf_op jit(solution)/shard_map/psum | solution.py:341
  261.7 7.6 %copy-start.56 = (pred[1024]{0:T(1024)(128)(4,1)S(1)}, pred[1024]{0:T(1024)(128)(4,1)}, u32[]{:S(2)}) copy-start(pred[1024]{0:T(1024)(128)(4,1)} %copy-done.55) | copy-start | bytes 3076
  333.1 6.4 copy-start.32
  335.5 10.2 %copy-start.31 = (bf16[2,512,4,64]{1,3,2,0:T(8,128)(2,1)S(1)}, bf16[2,512,4,64]{1,3,2,0:T(8,128)(2,1)}, u32[]{:S(2)}) copy-start(bf16[2,512,4,64]{1,3,2,0:T(8,128)(2,1)} %get-tuple-element.261) | copy-start | bytes 1572868
  357.7 10.1 %copy-start.54 = (pred[1024]{0:T(1024)(128)(4,1)S(1)}, pred[1024]{0:T(1024)(128)(4,1)}, u32[]{:S(2)}) copy-start(pred[1024]{0:T(1024)(128)(4,1)} %compare_and_fusion.1) | copy-start | bytes 3076
  367.9 6.9 %copy-start.19 = (bf16[1024,128]{1,0:T(8,128)(2,1)S(1)}, bf16[1024,128]{1,0:T(8,128)(2,1)}, u32[]{:S(2)}) copy-start(bf16[1024,128]{1,0:T(8,128)(2,1)} %copy-done.18) | copy-start | bytes 786436
  367.9 8.1 %copy-start.38 = (bf16[128,3,256]{2,0,1:T(8,128)(2,1)S(1)}, bf16[128,3,256]{2,0,1:T(8,128)(2,1)}, u32[]{:S(2)}) copy-start(bf16[128,3,256]{2,0,1:T(8,128)(2,1)} %param.49) | copy-start | bytes 589828
  375.9 110.1 %reduce-scatter.11.cloned.1.call-start = ((), (), s32[]{:S(2)}) async-start(), calls=%async_computation.10 | async-start | bytes 2949120 | tf_op jit(solution)/shard_map/reduce_scatter | solution.py:323
  381.7 246.6 %all-reduce.5.cloned.1.call-start = ((), (), s32[]{:S(2)}) async-start(), calls=%async_computation.11 | async-start | bytes 4194304 | tf_op jit(solution)/shard_map/psum | solution.py:336
  387.9 100.2 %copy-start.12 = (bf16[256,1024]{1,0:T(8,128)(2,1)S(1)}, bf16[256,1024]{1,0:T(8,128)(2,1)}, u32[]{:S(2)}) copy-start(bf16[256,1024]{1,0:T(8,128)(2,1)} %fusion.106) | copy-start | bytes 1572868
  454.5 34.9 %copy-start.3 = (bf16[256,1024]{1,0:T(8,128)(2,1)S(1)}, bf16[256,1024]{1,0:T(8,128)(2,1)}, u32[]{:S(2)}) copy-start(bf16[256,1024]{1,0:T(8,128)(2,1)} %param.31) | copy-start | bytes 1572868
  454.5 34.9 %copy-start.29 = (bf16[1024,128]{1,0:T(8,128)(2,1)S(1)}, bf16[1024,128]{1,0:T(8,128)(2,1)}, u32[]{:S(2)}) copy-start(bf16[1024,128]{1,0:T(8,128)(2,1)} %param.48) | copy-start | bytes 786436
  454.5 34.9 %copy-start.44 = (f32[256]{0:T(256)S(1)}, f32[256]{0:T(256)}, u32[]{:S(2)}) copy-start(f32[256]{0:T(256)} %copy-done.43) | copy-start | bytes 3076
  454.5 34.9 %copy-start.49 = (f32[1024]{0:T(1024)S(1)}, f32[1024]{0:T(1024)}, u32[]{:S(2)}) copy-start(f32[1024]{0:T(1024)} %param.36) | copy-start | bytes 12292
  458.2 33.1 %copy-start.62 = (f32[256]{0:T(256)S(1)}, f32[256]{0:T(256)}, u32[]{:S(2)}) copy-start(f32[256]{0:T(256)} %copy-done.61) | copy-start | bytes 3076
  458.2 33.1 %copy-start.53 = (f32[256]{0:T(256)S(1)}, f32[256]{0:T(256)}, u32[]{:S(2)}) copy-start(f32[256]{0:T(256)} %copy-done.52) | copy-start | bytes 3076
  491.7 143.1 %copy-start.1 = (bf16[1024,128]{1,0:T(8,128)(2,1)S(1)}, bf16[1024,128]{1,0:T(8,128)(2,1)}, u32[]{:S(2)}) copy-start(bf16[1024,128]{1,0:T(8,128)(2,1)} %param.52) | copy-start | bytes 786436
  (45 other events, 151.3 us)
Sparse Core Ops, SparseCore 0:
  12.2 26.6 all-gather.3
  89.5 33.0 reduce-scatter.4
  126.4 32.5 all-gather.5
  194.6 33.8 reduce-scatter.8
  233.3 23.4 all-gather.7
  259.3 33.1 reduce-scatter.6
  376.0 75.2 all-reduce.6
  453.8 32.0 reduce-scatter.10
  493.7 134.5 all-reduce.4
